TPU v7x, 32 devices: a whole 2x2x4 slice. The times are simulated.
32 devices in a mesh: shard: 2 (over y), tensor: 4 (over x, core), section: 4 (over z).
Axes of the slice: x: 2, y: 2, z: 4, core: 2. Of those that a mesh axis runs over, the one named last changes fastest.
Arguments:
- grad_parts: float32 [2, 4, 4, 1152, 1024], P('shard', 'tensor', 'section'), may hold values from -1 to 1
- master: float32 [1152, 16, 1024], P(('tensor', 'section'), 'shard'), may hold values from -0.1875 to 0.1875
- owner_map: int32 [4, 4], replicated, may hold values from 0 to 1, as said below
- left_factor: float32 [16, 1152, 1152], P('shard', ('tensor', 'section')), may hold values from -1.2 to 11.2, as said below
- right_factor: float32 [16, 1024, 1024], P('shard', ('tensor', 'section')), may hold values from -1.2 to 11.2, as said below
- left_basis: float32 [16, 1152, 1152], P('shard', ('tensor', 'section')), may hold values from -0.1875 to 0.1875
- right_basis: float32 [16, 1024, 1024], P('shard', None, ('tensor', 'section')), may hold values from -0.1875 to 0.1875
- moment_one: float32 [16, 1152, 1024], P('shard', ('tensor', 'section')), may hold values from -3 to 3
- moment_two: float32 [16, 1152, 1024], P('shard', ('tensor', 'section')), may hold values from 0.01 to 0.5
Outputs:
- new_master: float32 [1152, 16, 1024], P(('tensor', 'section'), 'shard')
- update_dir: float32 [1152, 16, 1024], P(('tensor', 'section'), 'shard')
- new_left: float32 [16, 1152, 1152], P('shard', ('tensor', 'section'))
- new_right: float32 [16, 1024, 1024], P('shard', ('tensor', 'section'))
- new_moment_one: float32 [16, 1152, 1024], P('shard', ('tensor', 'section'))
- new_moment_two: float32 [16, 1152, 1024], P('shard', ('tensor', 'section'))
Inputs may be any that keep to these rules, and one draw needn't show every extreme that they name: `owner_map`: each shard index owns exactly 8 matrices. `left_factor`: symmetric in its last two dimensions. `right_factor`: symmetric in its last two dimensions.
All inputs are finite; a program needn't handle non-finite values.
Results may differ from a plain program's by a relative error of at most 0.0003.
Values sent between devices are 32-bit elements; how exact they have to be, the bound alone decides.
A program may use at most 448 MiB of HBM per device.

v0:
```python
import jax
import jax.numpy as jnp
from jax import lax
from jax.sharding import PartitionSpec as P

beta_one = 0.95
beta_two = 0.95
epsilon = 1e-08
learn_rate = 0.01
decay_weight = 0.1
step_count = 10


def slot_table(owner_map, shards):
    owners_flat = owner_map.reshape(-1)
    matrices = owners_flat.shape[0]
    per_owner = matrices // shards
    member = (owners_flat[:, None] == jnp.arange(shards, dtype=jnp.int32)[None, :]).astype(
        jnp.int32
    )
    before = jnp.cumsum(member, axis=0) - member
    rank_in = jnp.sum(before * member, axis=1)
    slot_of = owners_flat * per_owner + rank_in
    places = (slot_of[:, None] == jnp.arange(matrices, dtype=jnp.int32)[None, :]).astype(jnp.int32)
    source = jnp.sum(places * jnp.arange(matrices, dtype=jnp.int32)[:, None], axis=0)
    return (slot_of, source)


def local(
    grad_parts,
    master,
    owner_map,
    left_factor,
    right_factor,
    left_basis,
    right_basis,
    moment_one,
    moment_two,
):
    exact_mode = lax.Precision.HIGHEST
    shards = lax.axis_size("shard")
    members = lax.axis_size(("tensor", "section"))
    position = lax.axis_index(("tensor", "section"))
    slot_of, source = slot_table(owner_map, shards)
    height = left_basis.shape[2]
    width = right_basis.shape[1]
    row_block = height // members
    col_block = width // members
    local_part = grad_parts[0, 0, 0]
    row_piece = lax.psum_scatter(local_part, "shard", scatter_dimension=0, tiled=True)
    stacked = lax.all_gather(row_piece[None], ("tensor", "section"), axis=0, tiled=True)
    ordered = jnp.take(stacked, source, axis=0)
    full_grad = lax.all_to_all(ordered, "shard", split_axis=0, concat_axis=1, tiled=True)
    full_right = lax.all_gather(right_basis, ("tensor", "section"), axis=2, tiled=True)
    grad_band = lax.dynamic_slice_in_dim(full_grad, position * row_block, row_block, 1)
    grad_slab = lax.dynamic_slice_in_dim(full_grad, position * col_block, col_block, 2)
    new_left = beta_two * left_factor + (1.0 - beta_two) * jnp.einsum(
        "orn,ofn->orf", grad_band, full_grad, precision=exact_mode
    )
    new_right = beta_two * right_factor + (1.0 - beta_two) * jnp.einsum(
        "ofc,ofn->ocn", grad_slab, full_grad, precision=exact_mode
    )
    turned = jnp.einsum("orf,ofn->orn", left_basis, full_grad, precision=exact_mode)
    rotated = jnp.einsum("orn,onk->ork", turned, full_right, precision=exact_mode)
    new_moment_one = beta_one * moment_one + (1.0 - beta_one) * rotated
    new_moment_two = beta_two * moment_two + (1.0 - beta_two) * rotated * rotated
    first_fix = 1.0 - beta_one**step_count
    second_fix = 1.0 - beta_two**step_count
    scaled = new_moment_one / first_fix / (jnp.sqrt(new_moment_two / second_fix) + epsilon)
    pulled = jnp.einsum("orn,okn->ork", scaled, full_right, precision=exact_mode)
    update_dir = lax.psum_scatter(
        jnp.einsum("orf,ork->fok", left_basis, pulled, precision=exact_mode),
        ("tensor", "section"),
        scatter_dimension=0,
        tiled=True,
    )
    new_master = master - learn_rate * (update_dir + decay_weight * master)
    return (new_master, update_dir, new_left, new_right, new_moment_one, new_moment_two)


def solution(mesh):
    placed = (
        P("shard", "tensor", "section", None, None),
        P(("tensor", "section"), "shard", None),
        P(),
        P("shard", ("tensor", "section"), None),
        P("shard", ("tensor", "section"), None),
        P("shard", ("tensor", "section"), None),
        P("shard", None, ("tensor", "section")),
        P("shard", ("tensor", "section"), None),
        P("shard", ("tensor", "section"), None),
    )
    return jax.shard_map(
        local,
        mesh=mesh,
        in_specs=placed,
        out_specs=(
            P(("tensor", "section"), "shard", None),
            P(("tensor", "section"), "shard", None),
            P("shard", ("tensor", "section"), None),
            P("shard", ("tensor", "section"), None),
            P("shard", ("tensor", "section"), None),
            P("shard", ("tensor", "section"), None),
        ),
        check_vma=False,
    )
```

profile of v0, /device:TPU:0, one launch (start us, length us, event | category | flops | bytes accessed | tf_op | source)
XLA Modules:
  0.0 1349.7 jit_solution(5164771268926579444)
XLA Ops:
  7.2 0.7 reduce-scatter.3.cloned.1.call-update
  7.9 0.0 all-gather.6.cloned.1.call-start
  8.0 65.1 %reduce-scatter.3.cloned.1.call-done = f32[576,1024]{1,0:T(8,128)} async-done(((f32[1152,1024]{1,0:T(8,128)}), f32[576,1024]{1,0:T(8,128)}) %reduce-scatter.3.cloned.1.call-update) | async-done | bytes 2359312 | tf_op jit(solution)/shard_map/reduce_scatter | solution.py:50
  73.1 0.0 all-gather.4.cloned.1.call-start
  73.1 0.7 all-gather.4.cloned.1.call-update
  73.8 0.0 reduce-scatter.5.cloned.1.call-start
  73.9 0.1 reshape.42
  73.9 0.1 fusion.15
  74.1 0.2 select_reduce_fusion.1
  74.2 0.1 select_reduce_fusion
  74.4 199.3 %all-gather.6.cloned.1.call-done = f32[9216,1024]{1,0:T(8,128)} async-done(((f32[576,1024]{1,0:T(8,128)}), f32[9216,1024]{1,0:T(8,128)}) %all-gather.6.cloned.1.call-update) | async-done | bytes 37748752 | tf_op jit(solution)/shard_map/all_gather | solution.py:51
  273.7 26.5 %gather_fusion = f32[16,576,1024]{2,1,0:T(8,128)} fusion(f32[16,576,1024]{2,1,0:T(8,128)} %bitcast.25, s32[1024]{0:T(1024)S(1)} %pad_clamp_fusion), kind=kCustom, calls=%fused_computation | custom fusion | bytes 75497536 | tf_op jit(solution)/shard_map/jit(_take)/gather | solution.py:52
  300.2 29.8 %broadcast_select_fusion = f32[16,576,1024]{2,1,0:T(8,128)} fusion(f32[16,576,1024]{2,1,0:T(8,128)} %gather_fusion, pred[16]{0:T(512)(128)(4,1)S(1)} %compare_and_fusion), kind=kLoop, calls=%fused_computation.2 | loop fusion | flops 9437184 | bytes 75497488 | tf_op jit(solution)/shard_map/jit(_take)/select_n | solution.py:52
  330.0 443.8 %all_to_all.18 = f32[16,576,1024]{2,1,0:T(8,128)} all-to-all(f32[16,576,1024]{2,1,0:T(8,128)} %broadcast_select_fusion), channel_id=1, replica_groups=mesh['shard'=2,'tensor'=4,'section'=4] {'shard'}, dimensions={0} | all-to-all | bytes 75497472 | tf_op jit(solution)/shard_map/all_to_all | solution.py:53
  773.9 28.0 %copy.29 = f32[8,2,576,1024]{3,2,1,0:T(8,128)} copy(f32[8,2,576,1024]{3,2,0,1:T(8,128)} %bitcast.24) | data formatting | bytes 75497472 | tf_op jit(solution)/shard_map/all_to_all | solution.py:53
  801.8 31.9 %fusion.21 = f32[8,1024,72]{1,2,0:T(8,128)} fusion(f32[8,1152,1024]{2,1,0:T(8,128)} %bitcast.21, f32[8,72,1152]{2,1,0:T(8,128)S(1)} %copy-done), kind=kOutput, calls=%fused_computation.36 | convolution fusion | flops 8153726976 | bytes 42762240 | tf_op jit(solution)/shard_map/orf,ofn->orn/dot_general | solution.py:63
  833.8 38.4 %multiply_add_fusion = (f32[8,72,1024]{2,1,0:T(8,128)}, f32[8,72,1024]{2,1,0:T(8,128)}) fusion(f32[8,72,1024]{2,1,0:T(8,128)} %param.16, f32[8,72,1024]{2,1,0:T(8,128)} %param.17, f32[8,1024,72]{1,2,0:T(8,128)} %fusion.21, f32[8,1024,1024]{1,2,0:T(8,128)} %all-gather.4.cloned.1.call-done), kind=kOutput, calls=%fused_computation.8 | convolution fusion | flops 7251296256 | bytes 45350912 | tf_op jit(solution)/shard_map/orn,onk->ork/dot_general | solution.py:64
  872.1 27.1 %fusion.5 = f32[8,72,1024]{2,1,0:T(8,128)} fusion(f32[8,1024,1024]{1,2,0:T(8,128)} %all-gather.4.cloned.1.call-done, f32[8,72,1024]{2,1,0:T(8,128)} %get-tuple-element.19, f32[8,72,1024]{2,1,0:T(8,128)} %get-tuple-element.18), kind=kOutput, calls=%fused_computation.12 | convolution fusion | flops 7250116608 | bytes 40632320 | tf_op jit(solution)/shard_map/orn,okn->ork/dot_general | solution.py:70
  899.2 34.9 %convolution_bitcast_fusion = f32[1152,8,1024]{0,2,1:T(8,128)} fusion(f32[8,72,1024]{2,1,0:T(8,128)} %fusion.5, f32[8,72,1152]{2,1,0:T(8,128)S(1)} %copy-done), kind=kOutput, calls=%fused_computation.1 | convolution fusion | flops 8153726976 | bytes 42762240 | tf_op jit(solution)/shard_map/orf,ork->fok/dot_general | solution.py:72
  934.1 37.2 %copy.30 = f32[1152,8,1024]{2,1,0:T(8,128)} copy(f32[1152,8,1024]{0,2,1:T(8,128)} %convolution_bitcast_fusion) | data formatting | bytes 75497472 | tf_op jit(solution)/shard_map/orf,ork->fok/transpose | solution.py:72
  971.3 43.8 %multiply_add_fusion.1 = f32[8,64,1024]{2,1,0:T(8,128)} fusion(f32[8,64,1024]{2,1,0:T(8,128)} %param.13, f32[8,1152,1024]{2,1,0:T(8,128)} %bitcast.22, s32[]{:T(128)S(6)} %select_n.30), kind=kOutput, calls=%fused_computation.18 | convolution fusion | flops 7249330176 | bytes 46661636 | tf_op jit(solution)/shard_map/ofc,ofn->ocn/dot_general | solution.py:60
  1015.2 42.9 %fusion.2 = f32[8,72,1152]{2,1,0:T(8,128)} fusion(f32[8,1152,1024]{2,1,0:T(8,128)} %bitcast.23, f32[8,72,1152]{2,1,0:T(8,128)S(1)} %copy-done.1, s32[]{:T(128)S(6)} %select_n.29), kind=kOutput, calls=%fused_computation.6 | convolution fusion | flops 8155717632 | bytes 45416452 | tf_op jit(solution)/shard_map/orn,ofn->orf/dot_general | solution.py:57
  1058.0 280.3 %reduce-scatter.5.cloned.1.call-done = f32[72,8,1024]{2,1,0:T(8,128)} async-done(((f32[1152,8,1024]{2,1,0:T(8,128)}), f32[72,8,1024]{2,1,0:T(8,128)}) %reduce-scatter.5.cloned.1.call-update) | async-done | bytes 2359312 | tf_op jit(solution)/shard_map/reduce_scatter | solution.py:71
  1338.4 4.6 multiply_subtract_fusion
  (15 shorter events, 0.2 us)
Async XLA Ops:
  7.2 794.7 %copy-start = (f32[8,72,1152]{2,1,0:T(8,128)S(1)}, f32[8,72,1152]{2,1,0:T(8,128)}, u32[]{:S(2)}) copy-start(f32[8,72,1152]{2,1,0:T(8,128)} %param.14) | copy-start | bytes 7962628
  7.2 65.9 %reduce-scatter.3.cloned.1.call-start = ((), (), s32[]{:S(2)}) async-start(), calls=%async_computation.3 | async-start | bytes 7077888 | tf_op jit(solution)/shard_map/reduce_scatter | solution.py:50
  7.9 65.9 %copy-start.2 = (s32[4,4]{1,0:T(4,128)S(1)}, s32[4,4]{1,0:T(4,128)}, u32[]{:S(2)}) copy-start(s32[4,4]{1,0:T(4,128)} %param.11) | copy-start | bytes 196
  7.9 265.8 %all-gather.6.cloned.1.call-start = ((), (), s32[]{:S(2)}) async-start(), calls=%async_computation.6 | async-start | bytes 40108032 | tf_op jit(solution)/shard_map/all_gather | solution.py:51
  73.1 760.7 %all-gather.4.cloned.1.call-start = ((), (), s32[]{:S(2)}) async-start(), calls=%async_computation.4 | async-start | bytes 35651584 | tf_op jit(solution)/shard_map/all_gather | solution.py:54
  73.8 1264.6 %reduce-scatter.5.cloned.1.call-start = ((), (), s32[]{:S(2)}) async-start(), calls=%async_computation.5 | async-start | bytes 40108032 | tf_op jit(solution)/shard_map/reduce_scatter | solution.py:71
  971.3 43.8 %copy-start.1 = (f32[8,72,1152]{2,1,0:T(8,128)S(1)}, f32[8,72,1152]{2,1,0:T(8,128)}, u32[]{:S(2)}) copy-start(f32[8,72,1152]{2,1,0:T(8,128)} %param.12) | copy-start | bytes 7962628
Sparse Core Ops, SparseCore 0:
  10.3 62.6 reduce-scatter.2
  74.7 198.9 all-gather.5
  275.3 177.9 all-gather.3
  971.4 366.8 reduce-scatter.4
where the time goes:
time: 1360 us; the launch traced here: 1350 us
  waiting for transfers between devices  546 us (40%)
  blocking collectives  444 us (33%)
  matrix products  219 us (16%)
  local copies, waits for them, and re-layouts  91.8 us (7%)
  other arithmetic  34.8 us (3%)
  between operations  14.1 us (1%)
    all_to_all x1, blocking collectives, local(): lax.all_to_all(ordered, 'shard', split_axis=0, concat_axis=1, tiled=True)  444 us
    reduce_scatter x1, waiting for transfers between devices, local(): lax.psum_scatter(jnp.einsum('orf,ork->fok', left_basis, pulled, precision...  280 us
    all_gather x1, waiting for transfers between devices, local(): lax.all_gather(row_piece[None], ('tensor', 'section'), axis=0, tiled=True)  199 us
    reduce_scatter x1, waiting for transfers between devices, local(): lax.psum_scatter(local_part, 'shard', scatter_dimension=0, tiled=True)  65.1 us
    dot_general x1, matrix products, local(): jnp.einsum('ofc,ofn->ocn', grad_slab, full_grad, precision=exact_mode)  43.8 us
    dot_general x1, matrix products, local(): jnp.einsum('orn,ofn->orf', grad_band, full_grad, precision=exact_mode)  42.9 us
    dot_general x1, matrix products, local(): jnp.einsum('orn,onk->ork', turned, full_right, precision=exact_mode)  38.4 us
    transpose x1, local copies, waits for them, and re-layouts, local(): jnp.einsum('orf,ork->fok', left_basis, pulled, precision=exact_mode)  37.2 us
  transfers between devices with their start and end apart: 4, of which 3 were waited for; matrix products, arithmetic and copies ran while one was open for 15% of the time, Pallas kernels for 0%

commit v1 on v0

--- a/solution.py
+++ b/solution.py
@@ -9,6 +9,12 @@
 learn_rate = 0.01
 decay_weight = 0.1
 step_count = 10
+
+
+def joined_along(tiles, dim):
+    tiles = jnp.moveaxis(tiles, 0, dim)
+    lengths = tiles.shape
+    return tiles.reshape(*lengths[:dim], lengths[dim] * lengths[dim + 1], *lengths[dim + 2 :])
 
 
 def slot_table(owner_map, shards):
@@ -48,7 +54,23 @@
     col_block = width // members
     local_part = grad_parts[0, 0, 0]
     row_piece = lax.psum_scatter(local_part, "shard", scatter_dimension=0, tiled=True)
-    stacked = lax.all_gather(row_piece[None], ("tensor", "section"), axis=0, tiled=True)
+    length = lax.axis_size(("tensor", "section"))
+    pairs = [(i, (i + 1) % length) for i in range(length)]
+    back = [(b, a) for a, b in pairs]
+    lower, upper = ([], [])
+    for step in range(length - 1):
+        if step % 2 == 0:
+            lower.append(
+                lax.ppermute(lower[-1] if lower else row_piece[None], ("tensor", "section"), pairs)
+            )
+        else:
+            upper.append(
+                lax.ppermute(upper[-1] if upper else row_piece[None], ("tensor", "section"), back)
+            )
+    blocks = jnp.stack([*lower[::-1], row_piece[None], *upper])
+    shift = lax.axis_index(("tensor", "section")) - len(lower)
+    blocks = blocks[(jnp.arange(length) - shift) % length]
+    stacked = joined_along(blocks, 0)
     ordered = jnp.take(stacked, source, axis=0)
     full_grad = lax.all_to_all(ordered, "shard", split_axis=0, concat_axis=1, tiled=True)
     full_right = lax.all_gather(right_basis, ("tensor", "section"), axis=2, tiled=True)

time: 1360 us -> 2070 us (1.52)
  waiting for transfers between devices: 546 us -> 1070 us
  starting transfers between devices: 0.15 us -> 120 us
  local copies, waits for them, and re-layouts: 91.8 us -> 163 us
    ppermute x0 -> x15, waiting for transfers between devices: none -> 719 us  [the longest x8 388 us: local(): lax.ppermute(lower[-1] if lower else row_piece[None], ('tensor', 'section...]
    all_gather x1 -> x0, waiting for transfers between devices: 199 us -> none  [local(): lax.all_gather(row_piece[None], ('tensor', 'section'), axis=0, tiled=True)]
    ppermute x0 -> x15, starting transfers between devices: none -> 119 us  [the longest x8 98.8 us: local(): lax.ppermute(lower[-1] if lower else row_piece[None], ('tensor', 'section...]
    unnamed x6 -> x63, local copies, waits for them, and re-layouts: 0.02 us -> 44.7 us
    gather x0 -> x1, local copies, waits for them, and re-layouts: none -> 25.7 us  [local(): blocks = blocks[(jnp.arange(length) - shift) % length]]
  transfers between devices with their start and end apart: 4 -> 18, of which waited for: 3 -> 16; matrix products, arithmetic and copies ran while one was open for 15% -> 13% of each run, Pallas kernels for 0% -> 0%
where the time goes in v1:
time: 2070 us; the launch traced here: 2060 us
  waiting for transfers between devices  1070 us (52%)
  blocking collectives  439 us (21%)
  matrix products  218 us (11%)
  local copies, waits for them, and re-layouts  163 us (8%)
  starting transfers between devices  120 us (6%)
  other arithmetic  34.3 us (2%)
    all_to_all x1, blocking collectives, local(): lax.all_to_all(ordered, 'shard', split_axis=0, concat_axis=1, tiled=True)  439 us
    ppermute x8, waiting for transfers between devices, local(): lax.ppermute(lower[-1] if lower else row_piece[None], ('tensor', 'section...  388 us
    ppermute x7, waiting for transfers between devices, local(): lax.ppermute(upper[-1] if upper else row_piece[None], ('tensor', 'section...  331 us
    reduce_scatter x1, waiting for transfers between devices, local(): lax.psum_scatter(jnp.einsum('orf,ork->fok', left_basis, pulled, precision...  284 us
    ppermute x8, starting transfers between devices, local(): lax.ppermute(lower[-1] if lower else row_piece[None], ('tensor', 'section...  98.8 us
    reduce_scatter x1, waiting for transfers between devices, local(): lax.psum_scatter(local_part, 'shard', scatter_dimension=0, tiled=True)  64.5 us
    unnamed x63, local copies, waits for them, and re-layouts  44.7 us
    dot_general x1, matrix products, local(): jnp.einsum('ofc,ofn->ocn', grad_slab, full_grad, precision=exact_mode)  43.4 us
  transfers between devices with their start and end apart: 18, of which 16 were waited for; matrix products, arithmetic and copies ran while one was open for 13% of the time, Pallas kernels for 0%

profile of v1, /device:TPU:0, one launch (start us, length us, event | category | flops | bytes accessed | tf_op | source)
XLA Modules:
  0.0 2058.7 jit_solution(16900289826286585545)
XLA Ops:
  9.4 64.5 %reduce-scatter.3.cloned.1.call-done = f32[576,1024]{1,0:T(8,128)} async-done(((f32[1152,1024]{1,0:T(8,128)}), f32[576,1024]{1,0:T(8,128)}) %reduce-scatter.3.cloned.1.call-update) | async-done | bytes 2359312 | tf_op jit(solution)/shard_map/reduce_scatter | solution.py:56
  75.4 80.2 %collective-permute-done = f32[1,576,1024]{2,1,0:T(8,128)S(1)} collective-permute-done((f32[1,576,1024]{2,1,0:T(8,128)}, f32[1,576,1024]{2,1,0:T(8,128)S(1)}, u32[]{:S(2)}, u32[]{:S(2)}) %collective-permute-start) | collective-permute-done | bytes 2359328 | tf_op jit(solution)/shard_map/ppermute | solution.py:64
  161.4 77.1 %collective-permute-done.1 = f32[1,576,1024]{2,1,0:T(8,128)S(1)} collective-permute-done((f32[1,576,1024]{2,1,0:T(8,128)S(1)}, f32[1,576,1024]{2,1,0:T(8,128)S(1)}, u32[]{:S(2)}, u32[]{:S(2)}) %collective-permute-start.1) | collective-permute-done | bytes 2359328 | tf_op jit(solution)/shard_map/ppermute | solution.py:64
  238.5 57.7 %collective-permute-done.8 = f32[1,576,1024]{2,1,0:T(8,128)S(1)} collective-permute-done((f32[1,576,1024]{2,1,0:T(8,128)}, f32[1,576,1024]{2,1,0:T(8,128)S(1)}, u32[]{:S(2)}, u32[]{:S(2)}) %collective-permute-start.8) | collective-permute-done | bytes 2359328 | tf_op jit(solution)/shard_map/ppermute | solution.py:68
  302.9 72.5 %collective-permute-done.2 = f32[1,576,1024]{2,1,0:T(8,128)S(1)} collective-permute-done((f32[1,576,1024]{2,1,0:T(8,128)S(1)}, f32[1,576,1024]{2,1,0:T(8,128)S(1)}, u32[]{:S(2)}, u32[]{:S(2)}) %collective-permute-start.2) | collective-permute-done | bytes 2359328 | tf_op jit(solution)/shard_map/ppermute | solution.py:64
  375.4 60.1 %collective-permute-done.9 = f32[1,576,1024]{2,1,0:T(8,128)S(1)} collective-permute-done((f32[1,576,1024]{2,1,0:T(8,128)S(1)}, f32[1,576,1024]{2,1,0:T(8,128)S(1)}, u32[]{:S(2)}, u32[]{:S(2)}) %collective-permute-start.9) | collective-permute-done | bytes 2359328 | tf_op jit(solution)/shard_map/ppermute | solution.py:68
  440.4 57.0 %collective-permute-done.3 = f32[1,576,1024]{2,1,0:T(8,128)S(1)} collective-permute-done((f32[1,576,1024]{2,1,0:T(8,128)S(1)}, f32[1,576,1024]{2,1,0:T(8,128)S(1)}, u32[]{:S(2)}, u32[]{:S(2)}) %collective-permute-start.3) | collective-permute-done | bytes 2359328 | tf_op jit(solution)/shard_map/ppermute | solution.py:64
  497.5 47.0 %collective-permute-done.10 = f32[1,576,1024]{2,1,0:T(8,128)S(1)} collective-permute-done((f32[1,576,1024]{2,1,0:T(8,128)S(1)}, f32[1,576,1024]{2,1,0:T(8,128)S(1)}, u32[]{:S(2)}, u32[]{:S(2)}) %collective-permute-start.10) | collective-permute-done | bytes 2359328 | tf_op jit(solution)/shard_map/ppermute | solution.py:68
  548.2 50.2 %collective-permute-done.4 = f32[1,576,1024]{2,1,0:T(8,128)S(1)} collective-permute-done((f32[1,576,1024]{2,1,0:T(8,128)S(1)}, f32[1,576,1024]{2,1,0:T(8,128)S(1)}, u32[]{:S(2)}, u32[]{:S(2)}) %collective-permute-start.4) | collective-permute-done | bytes 2359328 | tf_op jit(solution)/shard_map/ppermute | solution.py:64
  598.4 48.1 %collective-permute-start.5 = (f32[1,576,1024]{2,1,0:T(8,128)S(1)}, f32[1,576,1024]{2,1,0:T(8,128)S(1)}, u32[]{:S(2)}, u32[]{:S(2)}) collective-permute-start(f32[1,576,1024]{2,1,0:T(8,128)S(1)} %collective-permute-done.4), channel_id=1, source_target_pairs={{0,1},{1,2},{2,3},{3,4},{4,5},{5,6},{6,7},{7,8},{8,9},{9,10},{10,1... | collective-permute-start | bytes 7077896 | tf_op jit(solution)/shard_map/ppermute | solution.py:64
  653.3 50.0 %collective-permute-done.5 = f32[1,576,1024]{2,1,0:T(8,128)S(1)} collective-permute-done((f32[1,576,1024]{2,1,0:T(8,128)S(1)}, f32[1,576,1024]{2,1,0:T(8,128)S(1)}, u32[]{:S(2)}, u32[]{:S(2)}) %collective-permute-start.5) | collective-permute-done | bytes 2359328 | tf_op jit(solution)/shard_map/ppermute | solution.py:64
  703.3 47.1 %collective-permute-start.6 = (f32[1,576,1024]{2,1,0:T(8,128)S(1)}, f32[1,576,1024]{2,1,0:T(8,128)}, u32[]{:S(2)}, u32[]{:S(2)}) collective-permute-start(f32[1,576,1024]{2,1,0:T(8,128)S(1)} %collective-permute-done.5), channel_id=1, source_target_pairs={{0,1},{1,2},{2,3},{3,4},{4,5},{5,6},{6,7},{7,8},{8,9},{9,10},{10,1... | collective-permute-start | bytes 7077896 | tf_op jit(solution)/shard_map/ppermute | solution.py:64
  750.4 54.0 %collective-permute-done.12 = f32[1,576,1024]{2,1,0:T(8,128)} collective-permute-done((f32[1,576,1024]{2,1,0:T(8,128)S(1)}, f32[1,576,1024]{2,1,0:T(8,128)}, u32[]{:S(2)}, u32[]{:S(2)}) %collective-permute-start.12) | collective-permute-done | bytes 2359328 | tf_op jit(solution)/shard_map/ppermute | solution.py:68
  807.0 99.1 %collective-permute-done.13 = f32[1,576,1024]{2,1,0:T(8,128)} collective-permute-done((f32[1,576,1024]{2,1,0:T(8,128)}, f32[1,576,1024]{2,1,0:T(8,128)}, u32[]{:S(2)}, u32[]{:S(2)}) %collective-permute-start.13) | collective-permute-done | bytes 2359328 | tf_op jit(solution)/shard_map/ppermute | solution.py:68
  1010.5 29.3 %broadcast_select_fusion = f32[16,576,1024]{2,1,0:T(8,128)} fusion(f32[16,576,1024]{2,1,0:T(8,128)} %gather_fusion.1, pred[16]{0:T(512)(128)(4,1)S(1)} %compare_and_fusion), kind=kLoop, calls=%fused_computation.3 | loop fusion | flops 9437184 | bytes 75497488 | tf_op jit(solution)/shard_map/jit(_take)/select_n | solution.py:74
  1039.8 439.3 %all_to_all.18 = f32[16,576,1024]{2,1,0:T(8,128)} all-to-all(f32[16,576,1024]{2,1,0:T(8,128)} %broadcast_select_fusion), channel_id=1, replica_groups=mesh['shard'=2,'tensor'=4,'section'=4] {'shard'}, dimensions={0} | all-to-all | bytes 75497472 | tf_op jit(solution)/shard_map/all_to_all | solution.py:75
  1479.1 27.9 %copy.24 = f32[2,8,576,1024]{3,2,0,1:T(8,128)} copy(f32[2,8,576,1024]{3,2,1,0:T(8,128)} %bitcast.59) | data formatting | bytes 75497472 | tf_op jit(solution)/shard_map/all_to_all | solution.py:75
  1507.0 31.9 %fusion.23 = f32[8,1024,72]{1,2,0:T(8,128)} fusion(f32[8,1152,1024]{2,1,0:T(8,128)} %bitcast.56, f32[8,72,1152]{2,1,0:T(8,128)S(1)} %copy-done), kind=kOutput, calls=%fused_computation.60 | convolution fusion | flops 8153726976 | bytes 42762240 | tf_op jit(solution)/shard_map/orf,ofn->orn/dot_general | solution.py:85
  1539.0 38.4 %multiply_add_fusion = (f32[8,72,1024]{2,1,0:T(8,128)}, f32[8,72,1024]{2,1,0:T(8,128)}) fusion(f32[8,72,1024]{2,1,0:T(8,128)} %param.16, f32[8,72,1024]{2,1,0:T(8,128)} %param.17, f32[8,1024,72]{1,2,0:T(8,128)} %fusion.23, f32[8,1024,1024]{1,2,0:T(8,128)} %all-gather.2.cloned.1.call-done), kind=kOutput, calls=%fused_computation.9 | convolution fusion | flops 7251296256 | bytes 45350912 | tf_op jit(solution)/shard_map/orn,onk->ork/dot_general | solution.py:86
  1604.2 34.8 %convolution_bitcast_fusion = f32[1152,8,1024]{0,2,1:T(8,128)} fusion(f32[8,72,1024]{2,1,0:T(8,128)} %fusion.5, f32[8,72,1152]{2,1,0:T(8,128)S(1)} %copy-done), kind=kOutput, calls=%fused_computation.2 | convolution fusion | flops 8153726976 | bytes 42762240 | tf_op jit(solution)/shard_map/orf,ork->fok/dot_general | solution.py:94
  1639.0 37.3 %copy.25 = f32[1152,8,1024]{2,1,0:T(8,128)} copy(f32[1152,8,1024]{0,2,1:T(8,128)} %convolution_bitcast_fusion) | data formatting | bytes 75497472 | tf_op jit(solution)/shard_map/orf,ork->fok/transpose | solution.py:94
  1676.3 43.4 %multiply_add_fusion.1 = f32[8,64,1024]{2,1,0:T(8,128)} fusion(f32[8,64,1024]{2,1,0:T(8,128)} %param.13, f32[8,1152,1024]{2,1,0:T(8,128)} %bitcast.57, s32[]{:T(128)S(6)} %select_n.56), kind=kOutput, calls=%fused_computation.35 | convolution fusion | flops 7249330176 | bytes 46661636 | tf_op jit(solution)/shard_map/ofc,ofn->ocn/dot_general | solution.py:82
  1719.7 42.8 %fusion.2 = f32[8,72,1152]{2,1,0:T(8,128)} fusion(f32[8,1152,1024]{2,1,0:T(8,128)} %bitcast.58, f32[8,72,1152]{2,1,0:T(8,128)S(1)} %copy-done.1, s32[]{:T(128)S(6)} %select_n.55), kind=kOutput, calls=%fused_computation.7 | convolution fusion | flops 8155717632 | bytes 45416452 | tf_op jit(solution)/shard_map/orn,ofn->orf/dot_general | solution.py:79
  1762.5 284.0 %reduce-scatter.5.cloned.1.call-done = f32[72,8,1024]{2,1,0:T(8,128)} async-done(((f32[1152,8,1024]{2,1,0:T(8,128)}), f32[72,8,1024]{2,1,0:T(8,128)}) %reduce-scatter.5.cloned.1.call-update) | async-done | bytes 2359312 | tf_op jit(solution)/shard_map/reduce_scatter | solution.py:93
  (103 shorter events, 169.1 us)
Async XLA Ops:
  8.0 1499.0 %copy-start = (f32[8,72,1152]{2,1,0:T(8,128)S(1)}, f32[8,72,1152]{2,1,0:T(8,128)}, u32[]{:S(2)}) copy-start(f32[8,72,1152]{2,1,0:T(8,128)} %param.14) | copy-start | bytes 7962628
  8.0 65.9 %reduce-scatter.3.cloned.1.call-start = ((), (), s32[]{:S(2)}) async-start(), calls=%async_computation.3 | async-start | bytes 7077888 | tf_op jit(solution)/shard_map/reduce_scatter | solution.py:56
  8.1 798.4 %copy-start.23 = (s32[4,4]{1,0:T(4,128)S(1)}, s32[4,4]{1,0:T(4,128)}, u32[]{:S(2)}) copy-start(s32[4,4]{1,0:T(4,128)} %param.11) | copy-start | bytes 196
  8.7 1530.2 %all-gather.2.cloned.1.call-start = ((), (), s32[]{:S(2)}) async-start(), calls=%async_computation.4 | async-start | bytes 35651584 | tf_op jit(solution)/shard_map/all_gather | solution.py:76
  9.3 2037.2 %reduce-scatter.5.cloned.1.call-start = ((), (), s32[]{:S(2)}) async-start(), calls=%async_computation.5 | async-start | bytes 40108032 | tf_op jit(solution)/shard_map/reduce_scatter | solution.py:93
  73.9 81.7 %collective-permute-start = (f32[1,576,1024]{2,1,0:T(8,128)}, f32[1,576,1024]{2,1,0:T(8,128)S(1)}, u32[]{:S(2)}, u32[]{:S(2)}) collective-permute-start(f32[1,576,1024]{2,1,0:T(8,128)} %bitcast.61), channel_id=1, source_target_pairs={{0,1},{1,2},{2,3},{3,4},{4,5},{5,6},{6,7},{7,8},{8,9},{9,10},{10,1... | collective-permute-start | bytes 7077896 | tf_op jit(solution)/shard_map/ppermute | solution.py:64
  157.0 81.5 %collective-permute-start.1 = (f32[1,576,1024]{2,1,0:T(8,128)S(1)}, f32[1,576,1024]{2,1,0:T(8,128)S(1)}, u32[]{:S(2)}, u32[]{:S(2)}) collective-permute-start(f32[1,576,1024]{2,1,0:T(8,128)S(1)} %collective-permute-done), channel_id=1, source_target_pairs={{0,1},{1,2},{2,3},{3,4},{4,5},{5,6},{6,7},{7,8},{8,9},{9,10},{10,1... | collective-permute-start | bytes 7077896 | tf_op jit(solution)/shard_map/ppermute | solution.py:64
  157.0 139.2 %collective-permute-start.8 = (f32[1,576,1024]{2,1,0:T(8,128)}, f32[1,576,1024]{2,1,0:T(8,128)S(1)}, u32[]{:S(2)}, u32[]{:S(2)}) collective-permute-start(f32[1,576,1024]{2,1,0:T(8,128)} %bitcast.62), channel_id=1, source_target_pairs={{1,0},{2,1},{3,2},{4,3},{5,4},{6,5},{7,6},{8,7},{9,8},{10,9},{11,1... | collective-permute-start | bytes 7077896 | tf_op jit(solution)/shard_map/ppermute | solution.py:68
  238.5 197.1 %copy-start.7 = (f32[1,576,1024]{2,1,0:T(8,128)}, f32[1,576,1024]{2,1,0:T(8,128)S(1)}, u32[]{:S(2)}) copy-start(f32[1,576,1024]{2,1,0:T(8,128)S(1)} %collective-permute-done.1) | copy-start | bytes 7077892
  238.5 137.0 %collective-permute-start.2 = (f32[1,576,1024]{2,1,0:T(8,128)S(1)}, f32[1,576,1024]{2,1,0:T(8,128)S(1)}, u32[]{:S(2)}, u32[]{:S(2)}) collective-permute-start(f32[1,576,1024]{2,1,0:T(8,128)S(1)} %collective-permute-done.1), channel_id=1, source_target_pairs={{0,1},{1,2},{2,3},{3,4},{4,5},{5,6},{6,7},{7,8},{8,9},{9,10},{10,1... | collective-permute-start | bytes 7077896 | tf_op jit(solution)/shard_map/ppermute | solution.py:64
  297.7 137.8 %collective-permute-start.9 = (f32[1,576,1024]{2,1,0:T(8,128)S(1)}, f32[1,576,1024]{2,1,0:T(8,128)S(1)}, u32[]{:S(2)}, u32[]{:S(2)}) collective-permute-start(f32[1,576,1024]{2,1,0:T(8,128)S(1)} %collective-permute-done.8), channel_id=1, source_target_pairs={{1,0},{2,1},{3,2},{4,3},{5,4},{6,5},{7,6},{8,7},{9,8},{10,9},{11,1... | collective-permute-start | bytes 7077896 | tf_op jit(solution)/shard_map/ppermute | solution.py:68
  375.4 169.0 %copy-start.11 = (f32[1,576,1024]{2,1,0:T(8,128)}, f32[1,576,1024]{2,1,0:T(8,128)S(1)}, u32[]{:S(2)}) copy-start(f32[1,576,1024]{2,1,0:T(8,128)S(1)} %collective-permute-done.2) | copy-start | bytes 7077892
  375.4 122.0 %collective-permute-start.3 = (f32[1,576,1024]{2,1,0:T(8,128)S(1)}, f32[1,576,1024]{2,1,0:T(8,128)S(1)}, u32[]{:S(2)}, u32[]{:S(2)}) collective-permute-start(f32[1,576,1024]{2,1,0:T(8,128)S(1)} %collective-permute-done.2), channel_id=1, source_target_pairs={{0,1},{1,2},{2,3},{3,4},{4,5},{5,6},{6,7},{7,8},{8,9},{9,10},{10,1... | collective-permute-start | bytes 7077896 | tf_op jit(solution)/shard_map/ppermute | solution.py:64
  435.5 108.9 %collective-permute-start.10 = (f32[1,576,1024]{2,1,0:T(8,128)S(1)}, f32[1,576,1024]{2,1,0:T(8,128)S(1)}, u32[]{:S(2)}, u32[]{:S(2)}) collective-permute-start(f32[1,576,1024]{2,1,0:T(8,128)S(1)} %collective-permute-done.9), channel_id=1, source_target_pairs={{1,0},{2,1},{3,2},{4,3},{5,4},{6,5},{7,6},{8,7},{9,8},{10,9},{11,1... | collective-permute-start | bytes 7077896 | tf_op jit(solution)/shard_map/ppermute | solution.py:68
  497.5 306.9 %copy-start.17 = (f32[1,576,1024]{2,1,0:T(8,128)}, f32[1,576,1024]{2,1,0:T(8,128)S(1)}, u32[]{:S(2)}) copy-start(f32[1,576,1024]{2,1,0:T(8,128)S(1)} %collective-permute-done.3) | copy-start | bytes 7077892
  497.5 101.0 %collective-permute-start.4 = (f32[1,576,1024]{2,1,0:T(8,128)S(1)}, f32[1,576,1024]{2,1,0:T(8,128)S(1)}, u32[]{:S(2)}, u32[]{:S(2)}) collective-permute-start(f32[1,576,1024]{2,1,0:T(8,128)S(1)} %collective-permute-done.3), channel_id=1, source_target_pairs={{0,1},{1,2},{2,3},{3,4},{4,5},{5,6},{6,7},{7,8},{8,9},{9,10},{10,1... | collective-permute-start | bytes 7077896 | tf_op jit(solution)/shard_map/ppermute | solution.py:64
  544.5 105.0 %collective-permute-start.11 = (f32[1,576,1024]{2,1,0:T(8,128)S(1)}, f32[1,576,1024]{2,1,0:T(8,128)S(1)}, u32[]{:S(2)}, u32[]{:S(2)}) collective-permute-start(f32[1,576,1024]{2,1,0:T(8,128)S(1)} %collective-permute-done.10), channel_id=1, source_target_pairs={{1,0},{2,1},{3,2},{4,3},{5,4},{6,5},{7,6},{8,7},{9,8},{10,9},{11,1... | collective-permute-start | bytes 7077896 | tf_op jit(solution)/shard_map/ppermute | solution.py:68
  598.4 206.0 %copy-start.19 = (f32[1,576,1024]{2,1,0:T(8,128)}, f32[1,576,1024]{2,1,0:T(8,128)S(1)}, u32[]{:S(2)}) copy-start(f32[1,576,1024]{2,1,0:T(8,128)S(1)} %collective-permute-done.4) | copy-start | bytes 7077892
  598.4 104.8 %collective-permute-start.5 = (f32[1,576,1024]{2,1,0:T(8,128)S(1)}, f32[1,576,1024]{2,1,0:T(8,128)S(1)}, u32[]{:S(2)}, u32[]{:S(2)}) collective-permute-start(f32[1,576,1024]{2,1,0:T(8,128)S(1)} %collective-permute-done.4), channel_id=1, source_target_pairs={{0,1},{1,2},{2,3},{3,4},{4,5},{5,6},{6,7},{7,8},{8,9},{9,10},{10,1... | collective-permute-start | bytes 7077896 | tf_op jit(solution)/shard_map/ppermute | solution.py:64
  650.9 153.5 %collective-permute-start.12 = (f32[1,576,1024]{2,1,0:T(8,128)S(1)}, f32[1,576,1024]{2,1,0:T(8,128)}, u32[]{:S(2)}, u32[]{:S(2)}) collective-permute-start(f32[1,576,1024]{2,1,0:T(8,128)S(1)} %collective-permute-done.11), channel_id=1, source_target_pairs={{1,0},{2,1},{3,2},{4,3},{5,4},{6,5},{7,6},{8,7},{9,8},{10,9},{11,1... | collective-permute-start | bytes 7077896 | tf_op jit(solution)/shard_map/ppermute | solution.py:68
  703.3 101.1 %collective-permute-start.6 = (f32[1,576,1024]{2,1,0:T(8,128)S(1)}, f32[1,576,1024]{2,1,0:T(8,128)}, u32[]{:S(2)}, u32[]{:S(2)}) collective-permute-start(f32[1,576,1024]{2,1,0:T(8,128)S(1)} %collective-permute-done.5), channel_id=1, source_target_pairs={{0,1},{1,2},{2,3},{3,4},{4,5},{5,6},{6,7},{7,8},{8,9},{9,10},{10,1... | collective-permute-start | bytes 7077896 | tf_op jit(solution)/shard_map/ppermute | solution.py:64
  804.4 101.7 %collective-permute-start.13 = (f32[1,576,1024]{2,1,0:T(8,128)}, f32[1,576,1024]{2,1,0:T(8,128)}, u32[]{:S(2)}, u32[]{:S(2)}) collective-permute-start(f32[1,576,1024]{2,1,0:T(8,128)} %collective-permute-done.12), channel_id=1, source_target_pairs={{1,0},{2,1},{3,2},{4,3},{5,4},{6,5},{7,6},{8,7},{9,8},{10,9},{11,1... | collective-permute-start | bytes 7077896 | tf_op jit(solution)/shard_map/ppermute | solution.py:68
  804.4 102.6 %collective-permute-start.7 = (f32[1,576,1024]{2,1,0:T(8,128)}, f32[1,576,1024]{2,1,0:T(8,128)}, u32[]{:S(2)}, u32[]{:S(2)}) collective-permute-start(f32[1,576,1024]{2,1,0:T(8,128)} %collective-permute-done.6), channel_id=1, source_target_pairs={{0,1},{1,2},{2,3},{3,4},{4,5},{5,6},{6,7},{7,8},{8,9},{9,10},{10,1... | collective-permute-start | bytes 7077896 | tf_op jit(solution)/shard_map/ppermute | solution.py:64
  906.1 51.2 %collective-permute-start.14 = (f32[1,576,1024]{2,1,0:T(8,128)}, f32[1,576,1024]{2,1,0:T(8,128)S(1)}, u32[]{:S(2)}, u32[]{:S(2)}) collective-permute-start(f32[1,576,1024]{2,1,0:T(8,128)} %collective-permute-done.13), channel_id=1, source_target_pairs={{1,0},{2,1},{3,2},{4,3},{5,4},{6,5},{7,6},{8,7},{9,8},{10,9},{11,1... | collective-permute-start | bytes 7077896 | tf_op jit(solution)/shard_map/ppermute | solution.py:68
  (18 other events, 186.1 us)
Sparse Core Ops, SparseCore 0:
  11.1 62.7 reduce-scatter.2
Sparse Core Ops, SparseCore 1:
  10.8 498.7 all-gather.1
  1676.4 370.0 reduce-scatter.4
